TPU v7x, 512 devices: a whole 4x4x16 slice. The times are simulated.
512 devices in a mesh: loop: 64 (over z, x_hi, core), narrow: 8 (over x_lo, y).
Axes of the slice: x: 4 (x_hi: 2, x_lo: 2; x = x_hi * 2 + x_lo), y: 4, z: 16, core: 2. Of those that a mesh axis runs over, the one named last changes fastest.
Arguments:
- tokens: bfloat16 [1024, 8192], P('loop', 'narrow'), may hold values from -6 to 6
- gate_weight: bfloat16 [8192, 28672], P('narrow', 'loop'), may hold values from -0.0625 to 0.0625
- up_weight: bfloat16 [8192, 28672], P('narrow', 'loop'), may hold values from -0.0625 to 0.0625
- down_weight: bfloat16 [28672, 8192], P('loop', 'narrow'), may hold values from -0.03125 to 0.03125
Outputs:
- mixed: bfloat16 [1024, 8192], P('loop', 'narrow')
All inputs are finite; a program needn't handle non-finite values.
Results may differ from a plain program's by a relative error of at most 0.0049.
Values may be sent and summed in bfloat16 or wider, within the bound.
No kernel may reach another device: no remote copies, remote signals or barrier semaphores. Data moves between devices by JAX's collectives and lax.ppermute only.
A program may use at most 64 MiB of HBM per device.

v0:
```python
import jax
import jax.numpy as jnp
from jax import lax
from jax.sharding import PartitionSpec as P


def shards(tokens, gate_weight, up_weight, down_weight):
    width = gate_weight.shape[1]
    block_rows = lax.all_gather(tokens, "loop", axis=0, tiled=True)
    partial_sums = jnp.concatenate(
        (
            jnp.dot(block_rows, gate_weight, preferred_element_type=jnp.float32),
            jnp.dot(block_rows, up_weight, preferred_element_type=jnp.float32),
        ),
        axis=1,
    )
    totals = lax.psum(partial_sums, "narrow")
    hidden = (jax.nn.silu(totals[:, :width]) * totals[:, width:]).astype(jnp.bfloat16)
    mixed = lax.psum_scatter(
        jnp.dot(hidden, down_weight, preferred_element_type=jnp.float32),
        "loop",
        scatter_dimension=0,
        tiled=True,
    )
    return mixed.astype(jnp.bfloat16)


def solution(mesh):
    return jax.shard_map(
        shards,
        mesh=mesh,
        in_specs=(
            P("loop", "narrow"),
            P("narrow", "loop"),
            P("narrow", "loop"),
            P("loop", "narrow"),
        ),
        out_specs=P("loop", "narrow"),
        check_vma=False,
    )
```

profile of v0, /device:TPU:8, one launch (start us, length us, event | category | flops | bytes accessed | tf_op | source)
XLA Modules:
  0.0 507.0 jit_solution(5028401805543478411)
XLA Ops:
  6.5 0.0 copy-start
  6.5 0.0 all-gather.2.cloned.1.call-start
  6.5 0.7 all-gather.2.cloned.1.call-update
  7.3 0.0 copy-start.2
  7.3 0.0 all-reduce.2.cloned.1.call-start
  7.3 151.5 %all-gather.2.cloned.1.call-done = bf16[1024,1024]{1,0:T(8,128)(2,1)} async-done(((bf16[16,1024]{1,0:T(8,128)(2,1)}), bf16[1024,1024]{1,0:T(8,128)(2,1)}) %all-gather.2.cloned.1.call-update) | async-done | bytes 2097168 | tf_op jit(solution)/shard_map/all_gather | solution.py:9
  158.8 0.0 copy-start.1
  158.8 3.1 fusion.6
  162.0 0.0 copy-done.2
  162.0 0.0 copy-done.1
  162.0 1.2 fusion.5
  163.1 2.3 pad_maximum_fusion
  165.4 0.0 all-reduce.2.cloned.1.call-update
  165.4 0.0 reduce-scatter.2.cloned.1.call-start
  165.5 104.9 %all-reduce.2.cloned.1.call-done = f32[1024,896]{0,1:T(8,128)} async-done(((f32[1024,896]{0,1:T(8,128)}), f32[1024,896]{0,1:T(8,128)}) %all-reduce.2.cloned.1.call-update) | async-done | bytes 3670032 | tf_op jit(solution)/shard_map/psum | solution.py:17
  270.4 0.0 copy-done
  270.4 5.3 %fusion.1 = f32[1024,1024]{1,0:T(8,128)} fusion(bf16[448,1024]{1,0:T(8,128)(2,1)S(1)} %copy-done, f32[1024,896]{0,1:T(8,128)} %all-reduce.2.cloned.1.call-done), kind=kOutput, calls=%fused_computation.3 | convolution fusion | flops 942276608 | bytes 8781824 | tf_op jit(solution)/shard_map/dot_general | solution.py:20
  275.7 0.0 reduce-scatter.2.cloned.1.call-update
  275.8 223.2 %reduce-scatter.2.cloned.1.call-done = f32[16,1024]{1,0:T(8,128)} async-done(((f32[1024,1024]{1,0:T(8,128)}), f32[16,1024]{1,0:T(8,128)}) %reduce-scatter.2.cloned.1.call-update) | async-done | bytes 65552 | tf_op jit(solution)/shard_map/reduce_scatter | solution.py:19
  499.0 1.5 convert_element_type.7
Async XLA Ops:
  6.5 263.9 %copy-start = (bf16[448,1024]{1,0:T(8,128)(2,1)S(1)}, bf16[448,1024]{1,0:T(8,128)(2,1)}, u32[]{:S(2)}) copy-start(bf16[448,1024]{1,0:T(8,128)(2,1)} %param.7) | copy-start | bytes 2752516
  6.5 152.3 %all-gather.2.cloned.1.call-start = ((), (), s32[]{:S(2)}) async-start(), calls=%async_computation.1 | async-start | bytes 2129920 | tf_op jit(solution)/shard_map/all_gather | solution.py:9
  7.3 154.7 %copy-start.2 = (bf16[1024,448]{0,1:T(8,128)(2,1)S(1)}, bf16[1024,448]{0,1:T(8,128)(2,1)}, u32[]{:S(2)}) copy-start(bf16[1024,448]{0,1:T(8,128)(2,1)} %param.5) | copy-start | bytes 2752516
  7.3 263.1 %all-reduce.2.cloned.1.call-start = ((), (), s32[]{:S(2)}) async-start(), calls=%async_computation.2 | async-start | bytes 7340032 | tf_op jit(solution)/shard_map/psum | solution.py:17
  158.8 3.1 copy-start.1
  165.4 333.5 %reduce-scatter.2.cloned.1.call-start = ((), (), s32[]{:S(2)}) async-start(), calls=%async_computation.3 | async-start | bytes 4259840 | tf_op jit(solution)/shard_map/reduce_scatter | solution.py:19
Sparse Core Ops, SparseCore 0:
  10.7 148.1 all-gather.1
  165.6 104.7 all-reduce.1
  275.9 223.0 reduce-scatter.1
where the time goes:
time: 507 us
  waiting for transfers between devices  480 us (95%)
  between operations  13.1 us (3%)
  matrix products  9.59 us (2%)
    reduce_scatter x1, waiting for transfers between devices, shards(): lax.psum_scatter(jnp.dot(hidden, down_weight, preferred_element_type=jnp....  223 us
    all_gather x1, waiting for transfers between devices, shards(): block_rows = lax.all_gather(tokens, 'loop', axis=0, tiled=True)  152 us
    psum x1, waiting for transfers between devices, shards(): totals = lax.psum(partial_sums, 'narrow')  105 us
  transfers between devices with their start and end apart: 3, of which 3 were waited for; matrix products, arithmetic and copies ran while one was open for 0% of the time, Pallas kernels for 0%

commit v1 on v0

--- a/solution.py
+++ b/solution.py
@@ -4,9 +4,16 @@
 from jax.sharding import PartitionSpec as P
 
 
+def bring_chains_now(t0):
+    tile_out = jnp.stack([t0 for _ in range(jax.lax.axis_size("loop"))], axis=0)
+    current_value = jax.lax.all_to_all(tile_out, "loop", split_axis=0, concat_axis=0)
+    e_next = jnp.concatenate(current_value, axis=0)
+    return e_next
+
+
 def shards(tokens, gate_weight, up_weight, down_weight):
     width = gate_weight.shape[1]
-    block_rows = lax.all_gather(tokens, "loop", axis=0, tiled=True)
+    block_rows = bring_chains_now(tokens)
     partial_sums = jnp.concatenate(
         (
             jnp.dot(block_rows, gate_weight, preferred_element_type=jnp.float32),

time: 507 us -> 471 us (0.929)
  waiting for transfers between devices: 480 us -> 325 us
  blocking collectives: 0 us -> 120 us
    all_gather x1 -> x0, waiting for transfers between devices: 152 us -> none  [shards(): block_rows = lax.all_gather(tokens, 'loop', axis=0, tiled=True)]
    all_to_all x0 -> x1, blocking collectives: none -> 120 us  [bring_chains_now(): jax.lax.all_to_all(tile_out, 'loop', split_axis=0, concat_axis=0)]
  transfers between devices with their start and end apart: 3 -> 2, of which waited for: 3 -> 2; matrix products, arithmetic and copies ran while one was open for 0% -> 0% of each run, Pallas kernels for 0% -> 0%
where the time goes in v1:
time: 471 us; the launch traced here: 470 us
  waiting for transfers between devices  325 us (69%)
  blocking collectives  120 us (25%)
  between operations  13.4 us (3%)
  matrix products  7.62 us (2%)
    reduce_scatter x1, waiting for transfers between devices, shards(): lax.psum_scatter(jnp.dot(hidden, down_weight, preferred_element_type=jnp....  223 us
    all_to_all x1, blocking collectives, bring_chains_now(): jax.lax.all_to_all(tile_out, 'loop', split_axis=0, concat_axis=0)  120 us
    psum x1, waiting for transfers between devices, shards(): totals = lax.psum(partial_sums, 'narrow')  102 us
  transfers between devices with their start and end apart: 2, of which 2 were waited for; matrix products, arithmetic and copies ran while one was open for 0% of the time, Pallas kernels for 0%

profile of v1, /device:TPU:8, one launch (start us, length us, event | category | flops | bytes accessed | tf_op | source)
XLA Modules:
  0.0 470.4 jit_solution(14678517795647706684)
XLA Ops:
  6.5 0.0 copy-start
  6.5 0.0 all-reduce.2.cloned.1.call-start
  6.5 1.1 stack.2
  7.6 0.0 copy-start.1
  7.6 119.6 %all_to_all.5 = bf16[64,16,1024]{2,1,0:T(8,128)(2,1)S(1)} all-to-all(bf16[64,16,1024]{2,1,0:T(8,128)(2,1)S(1)} %stack.2), channel_id=1, replica_groups=mesh['loop'=64,'narrow'=8] {'loop'}, dimensions={0} | all-to-all | bytes 4194304 | tf_op jit(solution)/shard_map/all_to_all | solution.py:9
  127.2 0.0 copy-done.1
  127.2 0.0 copy-start.2
  127.2 1.1 fusion.6
  128.4 0.0 copy-done.2
  128.4 1.1 fusion.5
  129.6 2.3 pad_maximum_fusion
  131.8 0.0 all-reduce.2.cloned.1.call-update
  131.9 0.0 reduce-scatter.2.cloned.1.call-start
  131.9 101.5 %all-reduce.2.cloned.1.call-done = f32[1024,896]{0,1:T(8,128)} async-done(((f32[1024,896]{0,1:T(8,128)}), f32[1024,896]{0,1:T(8,128)}) %all-reduce.2.cloned.1.call-update) | async-done | bytes 3670032 | tf_op jit(solution)/shard_map/psum | solution.py:24
  233.5 0.0 copy-done
  233.5 5.3 %fusion.1 = f32[1024,1024]{1,0:T(8,128)} fusion(bf16[448,1024]{1,0:T(8,128)(2,1)S(1)} %copy-done, f32[1024,896]{0,1:T(8,128)} %all-reduce.2.cloned.1.call-done), kind=kOutput, calls=%fused_computation.3 | convolution fusion | flops 942276608 | bytes 8781824 | tf_op jit(solution)/shard_map/dot_general | solution.py:27
  238.8 0.0 reduce-scatter.2.cloned.1.call-update
  238.8 223.3 %reduce-scatter.2.cloned.1.call-done = f32[16,1024]{1,0:T(8,128)} async-done(((f32[1024,1024]{1,0:T(8,128)}), f32[16,1024]{1,0:T(8,128)}) %reduce-scatter.2.cloned.1.call-update) | async-done | bytes 65552 | tf_op jit(solution)/shard_map/reduce_scatter | solution.py:26
  462.1 1.5 convert_element_type.7
Async XLA Ops:
  6.5 226.9 %copy-start = (bf16[448,1024]{1,0:T(8,128)(2,1)S(1)}, bf16[448,1024]{1,0:T(8,128)(2,1)}, u32[]{:S(2)}) copy-start(bf16[448,1024]{1,0:T(8,128)(2,1)} %param.7) | copy-start | bytes 2752516
  6.5 226.9 %all-reduce.2.cloned.1.call-start = ((), (), s32[]{:S(2)}) async-start(), calls=%async_computation.2 | async-start | bytes 7340032 | tf_op jit(solution)/shard_map/psum | solution.py:24
  7.6 119.6 %copy-start.1 = (bf16[1024,448]{0,1:T(8,128)(2,1)S(1)}, bf16[1024,448]{0,1:T(8,128)(2,1)}, u32[]{:S(2)}) copy-start(bf16[1024,448]{0,1:T(8,128)(2,1)} %param.6) | copy-start | bytes 2752516
  127.2 1.2 copy-start.2
  131.9 330.2 %reduce-scatter.2.cloned.1.call-start = ((), (), s32[]{:S(2)}) async-start(), calls=%async_computation.3 | async-start | bytes 4259840 | tf_op jit(solution)/shard_map/reduce_scatter | solution.py:26
Sparse Core Ops, SparseCore 0:
  132.0 101.4 all-reduce.1
  238.9 223.1 reduce-scatter.1

commit v2 on v0

--- a/solution.py
+++ b/solution.py
@@ -2,6 +2,7 @@
 import jax.numpy as jnp
 from jax import lax
 from jax.sharding import PartitionSpec as P
+from jax.lax import all_gather
 
 
 def shards(tokens, gate_weight, up_weight, down_weight):
@@ -14,7 +15,7 @@
         ),
         axis=1,
     )
-    totals = lax.psum(partial_sums, "narrow")
+    totals = all_gather(partial_sums, "narrow").sum(axis=0)
     hidden = (jax.nn.silu(totals[:, :width]) * totals[:, width:]).astype(jnp.bfloat16)
     mixed = lax.psum_scatter(
         jnp.dot(hidden, down_weight, preferred_element_type=jnp.float32),

time: 507 us -> 729 us (1.44)
  waiting for transfers between devices: 480 us -> 664 us
  local copies, waits for them, and re-layouts: 0.01 us -> 30.8 us
  other arithmetic: 3.75 us -> 13.2 us
    all_gather x0 -> x1, waiting for transfers between devices: none -> 289 us  [shards(): totals = all_gather(partial_sums, 'narrow').sum(axis=0)]
    psum x1 -> x0, waiting for transfers between devices: 105 us -> none  [shards(): totals = lax.psum(partial_sums, 'narrow')]
    unnamed x6 -> x7, local copies, waits for them, and re-layouts: 0.01 us -> 30.8 us
    reduce_sum x0 -> x1, other arithmetic: none -> 9.43 us  [shards(): totals = all_gather(partial_sums, 'narrow').sum(axis=0)]
where the time goes in v2:
time: 729 us
  waiting for transfers between devices  664 us (91%)
  local copies, waits for them, and re-layouts  30.8 us (4%)
  other arithmetic  13.2 us (2%)
  between operations  13.2 us (2%)
  matrix products  7.56 us (1%)
    all_gather x1, waiting for transfers between devices, shards(): totals = all_gather(partial_sums, 'narrow').sum(axis=0)  289 us
    reduce_scatter x1, waiting for transfers between devices, shards(): lax.psum_scatter(jnp.dot(hidden, down_weight, preferred_element_type=jnp....  223 us
    all_gather x1, waiting for transfers between devices, shards(): block_rows = lax.all_gather(tokens, 'loop', axis=0, tiled=True)  152 us
    unnamed x7, local copies, waits for them, and re-layouts  30.8 us
  transfers between devices with their start and end apart: 3, of which 3 were waited for; matrix products, arithmetic and copies ran while one was open for 0% of the time, Pallas kernels for 0%

profile of v2, /device:TPU:8, one launch (start us, length us, event | category | flops | bytes accessed | tf_op | source)
XLA Modules:
  0.0 728.8 jit_solution(14918098127264116976)
XLA Ops:
  6.5 0.0 copy-start
  6.5 0.0 all-gather.4.cloned.1.call-start
  6.5 0.7 all-gather.4.cloned.1.call-update
  7.3 0.0 copy-start.2
  7.3 0.0 all-gather.6.cloned.1.call-start
  7.3 151.5 %all-gather.4.cloned.1.call-done = bf16[1024,1024]{1,0:T(8,128)(2,1)} async-done(((bf16[16,1024]{1,0:T(8,128)(2,1)}), bf16[1024,1024]{1,0:T(8,128)(2,1)}) %all-gather.4.cloned.1.call-update) | async-done | bytes 2097168 | tf_op jit(solution)/shard_map/all_gather | solution.py:10
  158.8 0.0 copy-start.1
  158.8 3.1 fusion.6
  162.0 0.0 copy-done.2
  162.0 0.0 copy-done.1
  162.0 1.2 fusion.5
  163.1 2.3 pad_maximum_fusion
  165.4 0.0 all-gather.6.cloned.1.call-update
  165.4 0.0 reduce-scatter.2.cloned.1.call-start
  165.5 288.5 %all-gather.6.cloned.1.call-done = f32[8192,896]{0,1:T(8,128)} async-done(((f32[1024,896]{0,1:T(8,128)}), f32[8192,896]{0,1:T(8,128)}) %all-gather.6.cloned.1.call-update) | async-done | bytes 29360144 | tf_op jit(solution)/shard_map/all_gather | solution.py:18
  454.0 30.8 %copy.5 = f32[112,8,8,1024]{3,2,1,0:T(8,128)S(1)} copy(f32[112,8,8,1024]{3,1,2,0:T(8,128)} %bitcast.10) | data formatting | bytes 58720256
  484.8 9.4 %bitcast_reduce_fusion = f32[1024,896]{0,1:T(8,128)S(1)} fusion(f32[112,8,8,1024]{3,2,1,0:T(8,128)S(1)} %copy.5), kind=kLoop, calls=%fused_computation | loop fusion | flops 6422528 | bytes 33030144 | tf_op jit(solution)/shard_map/reduce_sum | solution.py:18
  494.3 0.0 copy-done
  494.3 3.3 fusion.1
  497.6 0.0 reduce-scatter.2.cloned.1.call-update
  497.6 223.2 %reduce-scatter.2.cloned.1.call-done = f32[16,1024]{1,0:T(8,128)} async-done(((f32[1024,1024]{1,0:T(8,128)}), f32[16,1024]{1,0:T(8,128)}) %reduce-scatter.2.cloned.1.call-update) | async-done | bytes 65552 | tf_op jit(solution)/shard_map/reduce_scatter | solution.py:20
  720.8 1.5 convert_element_type.7
Async XLA Ops:
  6.5 487.7 %copy-start = (bf16[448,1024]{1,0:T(8,128)(2,1)S(1)}, bf16[448,1024]{1,0:T(8,128)(2,1)}, u32[]{:S(2)}) copy-start(bf16[448,1024]{1,0:T(8,128)(2,1)} %param.7) | copy-start | bytes 2752516
  6.5 152.3 %all-gather.4.cloned.1.call-start = ((), (), s32[]{:S(2)}) async-start(), calls=%async_computation.1 | async-start | bytes 2129920 | tf_op jit(solution)/shard_map/all_gather | solution.py:10
  7.3 154.7 %copy-start.2 = (bf16[1024,448]{0,1:T(8,128)(2,1)S(1)}, bf16[1024,448]{0,1:T(8,128)(2,1)}, u32[]{:S(2)}) copy-start(bf16[1024,448]{0,1:T(8,128)(2,1)} %param.5) | copy-start | bytes 2752516
  7.3 446.7 %all-gather.6.cloned.1.call-start = ((), (), s32[]{:S(2)}) async-start(), calls=%async_computation.3 | async-start | bytes 33030144 | tf_op jit(solution)/shard_map/all_gather | solution.py:18
  158.8 3.1 copy-start.1
  165.4 555.4 %reduce-scatter.2.cloned.1.call-start = ((), (), s32[]{:S(2)}) async-start(), calls=%async_computation.2 | async-start | bytes 4259840 | tf_op jit(solution)/shard_map/reduce_scatter | solution.py:20
Sparse Core Ops, SparseCore 0:
  10.7 148.1 all-gather.3
  165.6 288.4 all-gather.5
  497.7 223.0 reduce-scatter.1
